TPU v7x, 256 devices: a whole 4x4x8 slice. The times are simulated.
256 devices in a mesh: ctx: 16 (over y, x), exp: 16 (over z, core).
Axes of the slice: x: 4, y: 4, z: 8, core: 2. Of those that a mesh axis runs over, the one named last changes fastest.
Arguments:
- tokens: bfloat16 [2048, 4096], P('ctx', 'exp'), may hold values from -6 to 6
- input_weight: bfloat16 [4096, 8192], P('ctx', 'exp'), may hold values from -0.09375 to 0.09375
- gate_weight: bfloat16 [4096, 8192], P('ctx', 'exp'), may hold values from -0.09375 to 0.09375
- conv_weight: float32 [4, 8192], P(None, 'exp'), may hold values from -3 to 3
- conv_bias: float32 [8192], P('exp'), may hold values from -3 to 3
- state_weight: bfloat16 [8192, 32], P('exp'), may hold values from -0.0078125 to 0.0078125
- step_size: float32 [2048, 8192], P('ctx', 'exp'), may hold values from 0 to 1, as said below
- skip_gain: float32 [8192], P('exp'), may hold values from 0.5 to 2
- output_weight: bfloat16 [8192, 4096], P('exp', 'ctx'), may hold values from -0.0625 to 0.0625
- norm_gain: float32 [4096], replicated, may hold values from 0.1 to 1.9
- router_weight: bfloat16 [4096, 16], replicated, may hold values from -0.09375 to 0.09375
- expert_gate: bfloat16 [16, 7168, 4096], P('exp', 'ctx'), may hold values from -0.09375 to 0.09375
- expert_up: bfloat16 [16, 7168, 4096], P('exp', 'ctx'), may hold values from -0.09375 to 0.09375
- expert_down: bfloat16 [16, 7168, 4096], P('exp', 'ctx'), may hold values from -0.0625 to 0.0625
- expert_ids: int32 [2048, 2], P(('ctx', 'exp')), may hold values from 0 to 15, all different within a row; in each aligned block of 8 rows (0 to 7, 8 to 15, ...) at most 2 rows name the same one
Outputs:
- layer_out: bfloat16 [2048, 4096], P(('ctx', 'exp'))
Inputs may be any that keep to these rules, and one draw needn't show every extreme that they name: `expert_ids`: each token names 2 different experts; in each aligned block of 8 tokens no expert is named by more than 2 tokens. `step_size`: a positive rate for each token and channel.
All inputs are finite; a program needn't handle non-finite values.
Results may differ from a plain program's by a relative error of at most 0.028.
Values may be sent and summed in bfloat16 or wider, within the bound.
A program may use at most 128 MiB of HBM per device.

v0:
```python
import jax
import jax.numpy as jnp
from jax import lax
from jax.sharding import PartitionSpec as P

STATE = 16
CONV = 4
TOP = 2
CAP = 2
precise = lax.Precision.HIGHEST


def shifted(shard, axis, by):
    devices = lax.axis_size(axis)
    pairs = [(i, i + by) for i in range(devices) if 0 <= i + by < devices]
    return lax.ppermute(shard, axis, pairs)


def running_sum(values):
    length = values.shape[0]
    lower = jnp.tril(jnp.ones((length, length), jnp.float32))
    return jnp.dot(lower, values, precision=precise)


def causal_part(scores, decay_block, input_block):
    length = decay_block.shape[0]
    causal = (jnp.arange(length)[:, None] >= jnp.arange(length)[None, :])[:, :, None]
    distance = decay_block[:, None, :] - decay_block[None, :, :]
    weight = jnp.where(causal, jnp.exp(-jnp.where(causal, distance, 0.0)), 0.0)
    return jnp.einsum("ts,tsc,sc->tc", scores, weight, input_block, precision=precise)


def local(
    tokens,
    input_weight,
    gate_weight,
    conv_weight,
    conv_bias,
    state_weight,
    step_size,
    skip_gain,
    output_weight,
    norm_gain,
    router_weight,
    expert_gate,
    expert_up,
    expert_down,
    expert_ids,
):
    whole_stretch = lax.all_gather(tokens, "exp", axis=1, tiled=True)
    stretch_rows = whole_stretch.shape[0]
    inner_width = input_weight.shape[1]
    inner_x = jnp.dot(
        whole_stretch,
        lax.all_gather(input_weight, "ctx", axis=0, tiled=True),
        preferred_element_type=jnp.float32,
    )
    inner_z = jnp.dot(
        whole_stretch,
        lax.all_gather(gate_weight, "ctx", axis=0, tiled=True),
        preferred_element_type=jnp.float32,
    )
    inner_x = inner_x.astype(jnp.bfloat16)
    inner_z = inner_z.astype(jnp.bfloat16)
    earlier_rows = shifted(inner_x[stretch_rows - (CONV - 1) :], "ctx", 1)
    extended = jnp.concatenate([earlier_rows, inner_x], 0).astype(jnp.float32)
    filtered = jnp.broadcast_to(conv_bias[None, :], (stretch_rows, inner_width))
    for offset in range(CONV):
        filtered = (
            filtered + conv_weight[offset][None, :] * extended[offset : offset + stretch_rows]
        )
    mixer_in = jax.nn.silu(filtered).astype(jnp.bfloat16)
    mixer_wide = mixer_in.astype(jnp.float32)
    projections = lax.psum(
        jnp.dot(mixer_in, state_weight, preferred_element_type=jnp.float32), "exp"
    )
    input_gain = projections[:, :STATE]
    readout = projections[:, STATE:]
    cumulative = running_sum(step_size)
    scores = jnp.dot(readout, input_gain.T, precision=precise)
    block_width = 128
    block_count = inner_width // block_width
    decay_blocks = cumulative.reshape(stretch_rows, block_count, block_width).transpose(1, 0, 2)
    incoming_slabs = mixer_wide.reshape(stretch_rows, block_count, block_width).transpose(1, 0, 2)
    inside = lax.map(
        lambda paired: causal_part(scores, paired[0], paired[1]), (decay_blocks, incoming_slabs)
    )
    inside = inside.transpose(1, 0, 2).reshape(stretch_rows, inner_width)
    total_decay = cumulative[stretch_rows - 1]
    tail_weight = jnp.exp(-(total_decay[None, :] - cumulative)) * mixer_wide
    local_end = jnp.dot(tail_weight.T, input_gain, precision=precise)
    stretch_keep = jnp.exp(-total_decay)

    def relay_step(turn_index, received):
        leaving = stretch_keep[:, None] * received + local_end
        return shifted(leaving, "ctx", 1)

    entering = lax.fori_loop(0, lax.axis_size("ctx") - 1, relay_step, jnp.zeros_like(local_end))
    carried = jnp.exp(-cumulative) * jnp.dot(readout, entering.T, precision=precise)
    mixed_state = (inside + carried + skip_gain[None, :] * mixer_wide) * jax.nn.silu(
        inner_z.astype(jnp.float32)
    )
    blender_result = mixed_state.astype(jnp.bfloat16)
    row_count = expert_ids.shape[0]
    start_row = lax.axis_index("exp") * row_count
    own_tokens = lax.dynamic_slice_in_dim(whole_stretch, start_row, row_count, 0)
    out_whole = lax.all_gather(output_weight, "ctx", axis=1, tiled=True)
    projected = lax.psum_scatter(
        jnp.dot(blender_result, out_whole, preferred_element_type=jnp.float32).astype(jnp.bfloat16),
        "exp",
        scatter_dimension=0,
        tiled=True,
    ).astype(jnp.float32)
    residual = (own_tokens.astype(jnp.float32) + projected).astype(jnp.bfloat16)
    stream = residual.astype(jnp.float32)
    normed = (
        stream
        * lax.rsqrt(jnp.mean(stream * stream, -1, keepdims=True) + 1e-05)
        * norm_gain[None, :]
    ).astype(jnp.bfloat16)
    logits = jnp.dot(normed, router_weight, preferred_element_type=jnp.float32)
    experts = router_weight.shape[1]
    expert_range = jnp.arange(experts, dtype=jnp.int32)
    chosen = expert_ids[:, :, None] == expert_range[None, None, :]
    selected_entry = jnp.sum(jnp.where(chosen, logits[:, None, :], 0.0), -1)
    shares = jax.nn.sigmoid(selected_entry - selected_entry[:, ::-1])
    flat_hits = chosen.reshape(row_count * TOP, experts).astype(jnp.int32)
    earlier_hits = jnp.dot(
        jnp.tril(jnp.ones((row_count * TOP, row_count * TOP), jnp.float32), -1),
        flat_hits.astype(jnp.float32),
        precision=precise,
    ).astype(jnp.int32)
    slot_index = jnp.sum(earlier_hits * flat_hits, -1)
    target = expert_ids.reshape(-1) * CAP + slot_index
    placed = target[:, None] == jnp.arange(experts * CAP, dtype=jnp.int32)[None, :]
    placed = placed.reshape(row_count, TOP, experts * CAP)
    selector = jnp.any(placed, 1).astype(jnp.bfloat16)
    outgoing = lax.dot_general(
        selector, normed, (((0,), (0,)), ((), ())), preferred_element_type=jnp.float32
    ).astype(jnp.bfloat16)
    outgoing = outgoing.reshape(experts, CAP, -1)
    arrived = lax.all_to_all(outgoing, "exp", split_axis=0, concat_axis=0, tiled=True)
    arrived = arrived.reshape(-1, arrived.shape[2])
    gate_part = expert_gate[0]
    up_part = expert_up[0]
    down_part = expert_down[0]
    shard_rows = lax.all_gather(arrived, "ctx", axis=0, tiled=True)
    gate_value = lax.dot_general(
        shard_rows, gate_part, (((1,), (1,)), ((), ())), preferred_element_type=jnp.float32
    )
    up_value = lax.dot_general(
        shard_rows, up_part, (((1,), (1,)), ((), ())), preferred_element_type=jnp.float32
    )
    hidden = (jax.nn.silu(gate_value) * up_value).astype(jnp.bfloat16)
    partial_out = jnp.dot(hidden, down_part, preferred_element_type=jnp.float32)
    finished = lax.psum_scatter(
        partial_out.astype(jnp.bfloat16), "ctx", scatter_dimension=0, tiled=True
    )
    returned = lax.all_to_all(
        finished.reshape(experts, CAP, -1), "exp", split_axis=0, concat_axis=0, tiled=True
    )
    returned = returned.reshape(experts * CAP, -1).astype(jnp.float32)
    combine = jnp.sum(jnp.where(placed, shares[:, :, None], 0.0), 1)
    moe_out = jnp.dot(combine, returned, precision=precise)
    return (stream + moe_out).astype(jnp.bfloat16)


def solution(mesh):
    in_specs = (
        P("ctx", "exp"),
        P("ctx", "exp"),
        P("ctx", "exp"),
        P(None, "exp"),
        P("exp"),
        P("exp", None),
        P("ctx", "exp"),
        P("exp"),
        P("exp", "ctx"),
        P(),
        P(),
        P("exp", "ctx", None),
        P("exp", "ctx", None),
        P("exp", "ctx", None),
        P(("ctx", "exp"), None),
    )
    out_specs = P(("ctx", "exp"), None)
    return jax.shard_map(local, mesh=mesh, in_specs=in_specs, out_specs=out_specs, check_vma=False)
```

profile of v0, /device:TPU:1, one launch (start us, length us, event | category | flops | bytes accessed | tf_op | source)
XLA Modules:
  0.0 636.4 jit_solution(114218375562185634)
XLA Ops:
  10.6 40.3 %all-gather.6.cloned.1.call-done = bf16[128,4096]{1,0:T(8,128)(2,1)} async-done(((bf16[128,256]{1,0:T(8,128)(2,1)}), bf16[128,4096]{1,0:T(8,128)(2,1)}) %all-gather.6.cloned.1.call-update) | async-done | bytes 1048592 | tf_op jit(solution)/shard_map/all_gather | solution.py:50
  51.0 57.7 %all-gather.8.cloned.1.call-done = bf16[4096,512]{1,0:T(8,128)(2,1)} async-done(((bf16[256,512]{1,0:T(8,128)(2,1)}), bf16[4096,512]{1,0:T(8,128)(2,1)}) %all-gather.8.cloned.1.call-update) | async-done | bytes 4194320 | tf_op jit(solution)/shard_map/all_gather | solution.py:55
  115.1 52.4 %all-gather.10.cloned.1.call-done = bf16[4096,512]{1,0:T(8,128)(2,1)} async-done(((bf16[256,512]{1,0:T(8,128)(2,1)}), bf16[4096,512]{1,0:T(8,128)(2,1)}) %all-gather.10.cloned.1.call-update) | async-done | bytes 4194320 | tf_op jit(solution)/shard_map/all_gather | solution.py:60
  170.7 46.7 %psum.7 = f32[128,32]{0,1:T(8,128)S(1)} all-reduce(f32[128,32]{0,1:T(8,128)S(1)} %fusion.70), channel_id=1, replica_groups=mesh['ctx'=16,'exp'=16] {'exp'}, use_global_device_ids=true, to_apply=%region_0.1 | all-reduce | flops 4096 | bytes 32768 | tf_op jit(solution)/shard_map/psum | solution.py:74
  218.1 39.1 %while.20 = (s32[]{:T(128)}, f32[4,128,128]{2,1,0:T(8,128)S(1)}, f32[4,128,128]{2,1,0:T(8,128)S(1)}, f32[4,128,128]{2,1,0:T(8,128)S(1)}, f32[128,128]{1,0:T(8,128)S(1)}, /*index=5*/s32[]{:T(128)}) while((s32[]{:T(128)}, f32[4,128,128]{2,1,0:T(8,128)S(1)}, f32[4,128,128]{2,1,0:T(8,128)S(1)}, f32[4,128,128]{2,1,0:T(8,128)S(1)}, ...), condition=%wide.region_2.3_spmd, body=%wide.region_1.2_spmd.sunk | while | flops 35667968 | bytes 688205 | solution.py:85
  218.1 9.7 %fusion.104 = f32[128,1,128]{2,1,0:T(1,128)S(1)} fusion(f32[128,128,1]{1,2,0:T(1,128)S(1)} %bitcast.89, f32[128,128]{1,0:T(8,128)S(1)} %get-tuple-element.140, f32[128,128]{1,0:T(8,128)S(1)} %get-tuple-element.141, pred[128,128]{1,0:T(8,128)(4,1)S(1)} %iota_compare_fusion.10), kind=kOutput, calls=%fused_computation.clone.1 | convolution fusion | flops 35651584 | bytes 278528 | tf_op jit(solution)/shard_map/while/body/eval_jaxpr/ts,tsc,sc->tc/dot_general | solution.py:30
  227.9 9.7 %fusion.104 = f32[128,1,128]{2,1,0:T(1,128)S(1)} fusion(f32[128,128,1]{1,2,0:T(1,128)S(1)} %bitcast.89, f32[128,128]{1,0:T(8,128)S(1)} %get-tuple-element.140, f32[128,128]{1,0:T(8,128)S(1)} %get-tuple-element.141, pred[128,128]{1,0:T(8,128)(4,1)S(1)} %iota_compare_fusion.10), kind=kOutput, calls=%fused_computation.clone.1 | convolution fusion | flops 35651584 | bytes 278528 | tf_op jit(solution)/shard_map/while/body/eval_jaxpr/ts,tsc,sc->tc/dot_general | solution.py:30
  237.6 9.7 %fusion.104 = f32[128,1,128]{2,1,0:T(1,128)S(1)} fusion(f32[128,128,1]{1,2,0:T(1,128)S(1)} %bitcast.89, f32[128,128]{1,0:T(8,128)S(1)} %get-tuple-element.140, f32[128,128]{1,0:T(8,128)S(1)} %get-tuple-element.141, pred[128,128]{1,0:T(8,128)(4,1)S(1)} %iota_compare_fusion.10), kind=kOutput, calls=%fused_computation.clone.1 | convolution fusion | flops 35651584 | bytes 278528 | tf_op jit(solution)/shard_map/while/body/eval_jaxpr/ts,tsc,sc->tc/dot_general | solution.py:30
  247.4 9.7 %fusion.104 = f32[128,1,128]{2,1,0:T(1,128)S(1)} fusion(f32[128,128,1]{1,2,0:T(1,128)S(1)} %bitcast.89, f32[128,128]{1,0:T(8,128)S(1)} %get-tuple-element.140, f32[128,128]{1,0:T(8,128)S(1)} %get-tuple-element.141, pred[128,128]{1,0:T(8,128)(4,1)S(1)} %iota_compare_fusion.10), kind=kOutput, calls=%fused_computation.clone.1 | convolution fusion | flops 35651584 | bytes 278528 | tf_op jit(solution)/shard_map/while/body/eval_jaxpr/ts,tsc,sc->tc/dot_general | solution.py:30
  257.1 90.6 %while.21 = (s32[]{:T(128)}, f32[512,16]{0,1:T(8,128)S(1)}, f32[512]{0:T(512)S(1)}, f32[512,16]{0,1:T(8,128)S(1)}, s32[]{:T(128)}) while((s32[]{:T(128)}, f32[512,16]{0,1:T(8,128)S(1)}, f32[512]{0:T(512)S(1)}, f32[512,16]{0,1:T(8,128)S(1)}, s32[]{:T(128)}) %tuple.40), condition=%wide.region_4.5_spmd, body=%wide.region_3.4_spmd.sunk | while | flops 16386 | bytes 231525 | solution.py:98
  280.0 5.8 collective-permute-start
  293.5 5.8 collective-permute-start
  300.3 5.8 collective-permute-start
  307.1 5.8 collective-permute-start
  313.8 5.8 collective-permute-start
  320.6 5.8 collective-permute-start
  340.9 5.8 collective-permute-start
  352.9 81.1 %reduce-scatter.3.cloned.1.call-done = bf16[8,4096]{1,0:T(8,128)(2,1)} async-done(((bf16[128,4096]{1,0:T(8,128)(2,1)}), bf16[8,4096]{1,0:T(8,128)(2,1)}) %reduce-scatter.3.cloned.1.call-update) | async-done | bytes 65552 | tf_op jit(solution)/shard_map/reduce_scatter | solution.py:108
  435.4 19.1 %all_to_all.10 = bf16[16,2,4096]{2,1,0:T(2,128)(2,1)S(1)} all-to-all(bf16[16,2,4096]{2,1,0:T(2,128)(2,1)S(1)} %reshape.74), channel_id=1, replica_groups=mesh['ctx'=16,'exp'=16] {'exp'}, dimensions={0} | all-to-all | bytes 524288 | tf_op jit(solution)/shard_map/all_to_all | solution.py:142
  455.6 53.0 %all-gather.14.cloned.1.call-done = bf16[512,4096]{1,0:T(8,128)(2,1)} async-done(((bf16[32,4096]{1,0:T(8,128)(2,1)}), bf16[512,4096]{1,0:T(8,128)(2,1)}) %all-gather.14.cloned.1.call-update) | async-done | bytes 4194320 | tf_op jit(solution)/shard_map/all_gather | solution.py:147
  514.0 10.8 %convolution_convert_fusion = bf16[512,4096]{1,0:T(8,128)(2,1)} fusion(bf16[1,448,4096]{2,1,0:T(8,128)(2,1)} %param.32, bf16[512,4096]{1,0:T(8,128)(2,1)} %all-gather.14.cloned.1.call-done, bf16[1,448,4096]{2,1,0:T(8,128)(2,1)} %param.31, f32[512,448]{0,1:T(8,128)S(1)} %fusion.18), kind=kOutput, calls=%fused_computation.19 | convolution fusion | flops 3761569792 | bytes 16646144 | tf_op jit(solution)/shard_map/dot_general | solution.py:155
  524.8 80.9 %reduce-scatter.5.cloned.1.call-done = bf16[32,4096]{1,0:T(8,128)(2,1)} async-done(((bf16[512,4096]{1,0:T(8,128)(2,1)}), bf16[32,4096]{1,0:T(8,128)(2,1)}) %reduce-scatter.5.cloned.1.call-update) | async-done | bytes 262160 | tf_op jit(solution)/shard_map/reduce_scatter | solution.py:156
  607.5 9.4 %all-to-all-start.1 = ((bf16[16,2,4096]{2,1,0:T(2,128)(2,1)}), bf16[16,2,4096]{2,1,0:T(2,128)(2,1)S(1)}, u32[]{:S(2)}, u32[]{:S(2)}) async-start(bf16[16,2,4096]{2,1,0:T(2,128)(2,1)} %reshape.76), calls=%async_computation.3 | async-start | bytes 524288 | tf_op jit(solution)/shard_map/all_to_all | solution.py:159
  617.4 11.2 %all-to-all-done.1 = bf16[16,2,4096]{2,1,0:T(2,128)(2,1)S(1)} async-done(((bf16[16,2,4096]{2,1,0:T(2,128)(2,1)}), bf16[16,2,4096]{2,1,0:T(2,128)(2,1)S(1)}, u32[]{:S(2)}, u32[]{:S(2)}) %all-to-all-start.1) | async-done | bytes 262176 | tf_op jit(solution)/shard_map/all_to_all | solution.py:159
  (122 shorter events, 80.7 us)
Async XLA Ops:
  6.5 44.5 %all-gather.6.cloned.1.call-start = ((), (), s32[]{:S(2)}) async-start(), calls=%async_computation.4 | async-start | bytes 1114112 | tf_op jit(solution)/shard_map/all_gather | solution.py:50
  7.3 101.4 %all-gather.8.cloned.1.call-start = ((), (), s32[]{:S(2)}) async-start(), calls=%async_computation.5 | async-start | bytes 4456448 | tf_op jit(solution)/shard_map/all_gather | solution.py:55
  8.0 159.4 %all-gather.10.cloned.1.call-start = ((), (), s32[]{:S(2)}) async-start(), calls=%async_computation.6 | async-start | bytes 4456448 | tf_op jit(solution)/shard_map/all_gather | solution.py:60
  8.7 339.5 %all-gather.12.cloned.1.call-start = ((), (), s32[]{:S(2)}) async-start(), calls=%async_computation.7 | async-start | bytes 4456448 | tf_op jit(solution)/shard_map/all_gather | solution.py:107
  9.3 424.6 %reduce-scatter.3.cloned.1.call-start = ((), (), s32[]{:S(2)}) async-start(), calls=%async_computation.8 | async-start | bytes 1114112 | tf_op jit(solution)/shard_map/reduce_scatter | solution.py:108
  112.0 58.4 %collective-permute-start.1 = (bf16[3,512]{1,0:T(4,128)(2,1)S(1)}, bf16[3,512]{1,0:T(4,128)(2,1)S(1)}, u32[]{:S(2)}, u32[]{:S(2)}) collective-permute-start(bf16[3,512]{1,0:T(4,128)(2,1)S(1)} %slice.48), channel_id=1, source_target_pairs={{0,16},{16,32},{32,48},{48,64},{64,80},{80,96},{96,112},{112,128},... | collective-permute-start | bytes 9224 | tf_op jit(solution)/shard_map/ppermute | solution.py:16
  257.2 3.7 collective-permute-start
  260.9 4.7 collective-permute-start
  265.5 4.7 collective-permute-start
  270.2 5.1 collective-permute-start
  275.3 4.7 collective-permute-start
  280.0 6.9 %collective-permute-start = (f32[512,16]{0,1:T(8,128)S(1)}, f32[512,16]{0,1:T(8,128)S(1)}, u32[]{:S(2)}, u32[]{:S(2)}) collective-permute-start(f32[512,16]{0,1:T(8,128)S(1)} %multiply_add_fusion.3), channel_id=1, source_target_pairs={{0,16},{16,32},{32,48},{48,64},{64,80},{80,96},{96,112},{112,128},... | collective-permute-start | bytes 98312 | tf_op jit(solution)/shard_map/while/body/eval_jaxpr/ppermute | solution.py:16
  286.8 6.7 %collective-permute-start = (f32[512,16]{0,1:T(8,128)S(1)}, f32[512,16]{0,1:T(8,128)S(1)}, u32[]{:S(2)}, u32[]{:S(2)}) collective-permute-start(f32[512,16]{0,1:T(8,128)S(1)} %multiply_add_fusion.3), channel_id=1, source_target_pairs={{0,16},{16,32},{32,48},{48,64},{64,80},{80,96},{96,112},{112,128},... | collective-permute-start | bytes 98312 | tf_op jit(solution)/shard_map/while/body/eval_jaxpr/ppermute | solution.py:16
  293.5 6.8 %collective-permute-start = (f32[512,16]{0,1:T(8,128)S(1)}, f32[512,16]{0,1:T(8,128)S(1)}, u32[]{:S(2)}, u32[]{:S(2)}) collective-permute-start(f32[512,16]{0,1:T(8,128)S(1)} %multiply_add_fusion.3), channel_id=1, source_target_pairs={{0,16},{16,32},{32,48},{48,64},{64,80},{80,96},{96,112},{112,128},... | collective-permute-start | bytes 98312 | tf_op jit(solution)/shard_map/while/body/eval_jaxpr/ppermute | solution.py:16
  300.3 6.8 %collective-permute-start = (f32[512,16]{0,1:T(8,128)S(1)}, f32[512,16]{0,1:T(8,128)S(1)}, u32[]{:S(2)}, u32[]{:S(2)}) collective-permute-start(f32[512,16]{0,1:T(8,128)S(1)} %multiply_add_fusion.3), channel_id=1, source_target_pairs={{0,16},{16,32},{32,48},{48,64},{64,80},{80,96},{96,112},{112,128},... | collective-permute-start | bytes 98312 | tf_op jit(solution)/shard_map/while/body/eval_jaxpr/ppermute | solution.py:16
  307.1 6.8 %collective-permute-start = (f32[512,16]{0,1:T(8,128)S(1)}, f32[512,16]{0,1:T(8,128)S(1)}, u32[]{:S(2)}, u32[]{:S(2)}) collective-permute-start(f32[512,16]{0,1:T(8,128)S(1)} %multiply_add_fusion.3), channel_id=1, source_target_pairs={{0,16},{16,32},{32,48},{48,64},{64,80},{80,96},{96,112},{112,128},... | collective-permute-start | bytes 98312 | tf_op jit(solution)/shard_map/while/body/eval_jaxpr/ppermute | solution.py:16
  313.8 6.8 %collective-permute-start = (f32[512,16]{0,1:T(8,128)S(1)}, f32[512,16]{0,1:T(8,128)S(1)}, u32[]{:S(2)}, u32[]{:S(2)}) collective-permute-start(f32[512,16]{0,1:T(8,128)S(1)} %multiply_add_fusion.3), channel_id=1, source_target_pairs={{0,16},{16,32},{32,48},{48,64},{64,80},{80,96},{96,112},{112,128},... | collective-permute-start | bytes 98312 | tf_op jit(solution)/shard_map/while/body/eval_jaxpr/ppermute | solution.py:16
  320.6 6.9 %collective-permute-start = (f32[512,16]{0,1:T(8,128)S(1)}, f32[512,16]{0,1:T(8,128)S(1)}, u32[]{:S(2)}, u32[]{:S(2)}) collective-permute-start(f32[512,16]{0,1:T(8,128)S(1)} %multiply_add_fusion.3), channel_id=1, source_target_pairs={{0,16},{16,32},{32,48},{48,64},{64,80},{80,96},{96,112},{112,128},... | collective-permute-start | bytes 98312 | tf_op jit(solution)/shard_map/while/body/eval_jaxpr/ppermute | solution.py:16
  327.6 6.6 %collective-permute-start = (f32[512,16]{0,1:T(8,128)S(1)}, f32[512,16]{0,1:T(8,128)S(1)}, u32[]{:S(2)}, u32[]{:S(2)}) collective-permute-start(f32[512,16]{0,1:T(8,128)S(1)} %multiply_add_fusion.3), channel_id=1, source_target_pairs={{0,16},{16,32},{32,48},{48,64},{64,80},{80,96},{96,112},{112,128},... | collective-permute-start | bytes 98312 | tf_op jit(solution)/shard_map/while/body/eval_jaxpr/ppermute | solution.py:16
  334.2 6.8 %collective-permute-start = (f32[512,16]{0,1:T(8,128)S(1)}, f32[512,16]{0,1:T(8,128)S(1)}, u32[]{:S(2)}, u32[]{:S(2)}) collective-permute-start(f32[512,16]{0,1:T(8,128)S(1)} %multiply_add_fusion.3), channel_id=1, source_target_pairs={{0,16},{16,32},{32,48},{48,64},{64,80},{80,96},{96,112},{112,128},... | collective-permute-start | bytes 98312 | tf_op jit(solution)/shard_map/while/body/eval_jaxpr/ppermute | solution.py:16
  340.9 6.8 %collective-permute-start = (f32[512,16]{0,1:T(8,128)S(1)}, f32[512,16]{0,1:T(8,128)S(1)}, u32[]{:S(2)}, u32[]{:S(2)}) collective-permute-start(f32[512,16]{0,1:T(8,128)S(1)} %multiply_add_fusion.3), channel_id=1, source_target_pairs={{0,16},{16,32},{32,48},{48,64},{64,80},{80,96},{96,112},{112,128},... | collective-permute-start | bytes 98312 | tf_op jit(solution)/shard_map/while/body/eval_jaxpr/ppermute | solution.py:16
  352.1 156.4 %all-gather.14.cloned.1.call-start = ((), (), s32[]{:S(2)}) async-start(), calls=%async_computation.9 | async-start | bytes 4456448 | tf_op jit(solution)/shard_map/all_gather | solution.py:147
  455.3 150.3 %reduce-scatter.5.cloned.1.call-start = ((), (), s32[]{:S(2)}) async-start(), calls=%async_computation.10 | async-start | bytes 4456448 | tf_op jit(solution)/shard_map/reduce_scatter | solution.py:156
  607.5 21.1 %all-to-all-start.1 = ((bf16[16,2,4096]{2,1,0:T(2,128)(2,1)}), bf16[16,2,4096]{2,1,0:T(2,128)(2,1)S(1)}, u32[]{:S(2)}, u32[]{:S(2)}) async-start(bf16[16,2,4096]{2,1,0:T(2,128)(2,1)} %reshape.76), calls=%async_computation.3 | async-start | bytes 524288 | tf_op jit(solution)/shard_map/all_to_all | solution.py:159
  (8 other events, 550.8 us)
Sparse Core Ops, SparseCore 0:
  9.1 41.8 all-gather.5
  53.4 55.2 all-gather.7
  111.1 56.2 all-gather.9
  169.7 61.4 all-gather.11
  352.3 81.6 reduce-scatter.2
  455.4 53.0 all-gather.13
  524.9 80.7 reduce-scatter.4
where the time goes:
time: 637 us; the launch traced here: 636 us
  waiting for transfers between devices  394 us (62%)
  starting transfers between devices  87.9 us (14%)
  matrix products  68.1 us (11%)
  blocking collectives  65.7 us (10%)
  between operations  13.7 us (2%)
    reduce_scatter x1, waiting for transfers between devices, local(): lax.psum_scatter(jnp.dot(blender_result, out_whole, preferred_element_typ...  81.1 us
    reduce_scatter x1, waiting for transfers between devices, local(): lax.psum_scatter(partial_out.astype(jnp.bfloat16), 'ctx', scatter_dimensi...  80.9 us
    ppermute x16, starting transfers between devices, shifted(): return lax.ppermute(shard, axis, pairs)  78.2 us
    all_gather x1, waiting for transfers between devices, local(): lax.all_gather(input_weight, 'ctx', axis=0, tiled=True)  57.7 us
    all_gather x1, waiting for transfers between devices, local(): shard_rows = lax.all_gather(arrived, 'ctx', axis=0, tiled=True)  53 us
    all_gather x1, waiting for transfers between devices, local(): lax.all_gather(gate_weight, 'ctx', axis=0, tiled=True)  52.4 us
    psum x1, blocking collectives, local(): lax.psum(jnp.dot(mixer_in, state_weight, preferred_element_type=jnp.float...  46.7 us
    all_gather x1, waiting for transfers between devices, local(): whole_stretch = lax.all_gather(tokens, 'exp', axis=1, tiled=True)  40.3 us
  transfers between devices with their start and end apart: 24, of which 22 were waited for; matrix products, arithmetic and copies ran while one was open for 8% of the time, Pallas kernels for 0%

commit v1 on v0

--- a/solution.py
+++ b/solution.py
@@ -8,6 +8,28 @@
 TOP = 2
 CAP = 2
 precise = lax.Precision.HIGHEST
+
+
+def in_order(tiles, dim):
+    tiles = jnp.moveaxis(tiles, 0, dim)
+    lengths = tiles.shape
+    return tiles.reshape(*lengths[:dim], lengths[dim] * lengths[dim + 1], *lengths[dim + 2 :])
+
+
+def ring_gather(x, axis, dim):
+    size = lax.axis_size(axis)
+    pairs = [(i, (i + 1) % size) for i in range(size)]
+    back = [(b, a) for a, b in pairs]
+    lower, upper = ([], [])
+    for hop in range(size - 1):
+        if hop % 2 == 0:
+            lower.append(lax.ppermute(lower[-1] if lower else x, axis, pairs))
+        else:
+            upper.append(lax.ppermute(upper[-1] if upper else x, axis, back))
+    blocks = jnp.stack([*lower[::-1], x, *upper])
+    shift = lax.axis_index(axis) - len(lower)
+    blocks = blocks[(jnp.arange(size) - shift) % size]
+    return in_order(blocks, dim)
 
 
 def shifted(shard, axis, by):
@@ -51,9 +73,7 @@
     stretch_rows = whole_stretch.shape[0]
     inner_width = input_weight.shape[1]
     inner_x = jnp.dot(
-        whole_stretch,
-        lax.all_gather(input_weight, "ctx", axis=0, tiled=True),
-        preferred_element_type=jnp.float32,
+        whole_stretch, ring_gather(input_weight, "ctx", 0), preferred_element_type=jnp.float32
     )
     inner_z = jnp.dot(
         whole_stretch,

time: 637 us -> 587 us (0.922)
  waiting for transfers between devices: 394 us -> 287 us
  starting transfers between devices: 87.9 us -> 118 us
  local copies, waits for them, and re-layouts: 4.31 us -> 20.9 us
  blocking collectives: 65.7 us -> 75.2 us
    all_gather x1 -> x0, waiting for transfers between devices: 57.7 us -> none  [local(): lax.all_gather(input_weight, 'ctx', axis=0, tiled=True)]
    all_gather x1, waiting for transfers between devices: 52.4 us -> 0.02 us  [local(): lax.all_gather(gate_weight, 'ctx', axis=0, tiled=True)]
    ppermute x0 -> x15, waiting for transfers between devices: none -> 41.3 us  [the longest x8 41.3 us: ring_gather(): lower.append(lax.ppermute(lower[-1] if lower else x, axis, pairs))]
    all_gather x1, waiting for transfers between devices: 40.3 us -> 0.01 us  [local(): whole_stretch = lax.all_gather(tokens, 'exp', axis=1, tiled=True)]
    ppermute x0 -> x15, starting transfers between devices: none -> 37.3 us  [the longest x7 35.1 us: ring_gather(): upper.append(lax.ppermute(upper[-1] if upper else x, axis, back))]
    unnamed x17 -> x34, local copies, waits for them, and re-layouts: 0.12 us -> 11 us
    psum x1, blocking collectives: 46.7 us -> 56.1 us  [local(): lax.psum(jnp.dot(mixer_in, state_weight, preferred_element_type=jnp.float...]
    ppermute x16, starting transfers between devices: 78.2 us -> 71.4 us  [shifted(): return lax.ppermute(shard, axis, pairs)]
  transfers between devices with their start and end apart: 24 -> 38, of which waited for: 22 -> 28; matrix products, arithmetic and copies ran while one was open for 8% -> 11% of each run, Pallas kernels for 0% -> 0%
where the time goes in v1:
time: 587 us; the launch traced here: 586 us
  waiting for transfers between devices  287 us (49%)
  starting transfers between devices  118 us (20%)
  blocking collectives  75.2 us (13%)
  matrix products  68.2 us (12%)
  local copies, waits for them, and re-layouts  20.9 us (4%)
  between operations  13.8 us (2%)
    reduce_scatter x1, waiting for transfers between devices, local(): lax.psum_scatter(jnp.dot(blender_result, out_whole, preferred_element_typ...  83.1 us
    reduce_scatter x1, waiting for transfers between devices, local(): lax.psum_scatter(partial_out.astype(jnp.bfloat16), 'ctx', scatter_dimensi...  80.9 us
    ppermute x16, starting transfers between devices, shifted(): return lax.ppermute(shard, axis, pairs)  71.4 us
    psum x1, blocking collectives, local(): lax.psum(jnp.dot(mixer_in, state_weight, preferred_element_type=jnp.float...  56.1 us
    all_gather x1, waiting for transfers between devices, local(): shard_rows = lax.all_gather(arrived, 'ctx', axis=0, tiled=True)  53.1 us
    ppermute x8, waiting for transfers between devices, ring_gather(): lower.append(lax.ppermute(lower[-1] if lower else x, axis, pairs))  41.3 us
    dot_general x4, matrix products, causal_part(): jnp.einsum('ts,tsc,sc->tc', scores, weight, input_block, precision=precise)  38.7 us
    ppermute x7, starting transfers between devices, ring_gather(): upper.append(lax.ppermute(upper[-1] if upper else x, axis, back))  35.1 us
  transfers between devices with their start and end apart: 38, of which 28 were waited for; matrix products, arithmetic and copies ran while one was open for 11% of the time, Pallas kernels for 0%

profile of v1, /device:TPU:1, one launch (start us, length us, event | category | flops | bytes accessed | tf_op | source)
XLA Modules:
  0.0 585.8 jit_solution(6544480303606472909)
XLA Ops:
  10.2 8.0 %collective-permute-done.1 = bf16[256,512]{1,0:T(8,128)(2,1)S(1)} collective-permute-done((bf16[256,512]{1,0:T(8,128)(2,1)}, bf16[256,512]{1,0:T(8,128)(2,1)S(1)}, u32[]{:S(2)}, u32[]{:S(2)}) %collective-permute-start.1) | collective-permute-done | bytes 262176 | tf_op jit(solution)/shard_map/ppermute | solution.py:26
  68.0 8.2 %collective-permute-done.7 = bf16[256,512]{1,0:T(8,128)(2,1)S(1)} collective-permute-done((bf16[256,512]{1,0:T(8,128)(2,1)S(1)}, bf16[256,512]{1,0:T(8,128)(2,1)S(1)}, u32[]{:S(2)}, u32[]{:S(2)}) %collective-permute-start.7) | collective-permute-done | bytes 262176 | tf_op jit(solution)/shard_map/ppermute | solution.py:26
  82.1 5.9 %collective-permute-done.8 = bf16[256,512]{1,0:T(8,128)(2,1)S(1)} collective-permute-done((bf16[256,512]{1,0:T(8,128)(2,1)S(1)}, bf16[256,512]{1,0:T(8,128)(2,1)S(1)}, u32[]{:S(2)}, u32[]{:S(2)}) %collective-permute-start.8) | collective-permute-done | bytes 262176 | tf_op jit(solution)/shard_map/ppermute | solution.py:26
  110.4 56.1 %psum.7 = f32[128,32]{0,1:T(8,128)S(1)} all-reduce(f32[128,32]{0,1:T(8,128)S(1)} %fusion.73), channel_id=1, replica_groups=mesh['ctx'=16,'exp'=16] {'exp'}, use_global_device_ids=true, to_apply=%region_0.1 | all-reduce | flops 4096 | bytes 32768 | tf_op jit(solution)/shard_map/psum | solution.py:94
  167.1 39.1 %while.20 = (s32[]{:T(128)}, f32[4,128,128]{2,1,0:T(8,128)S(1)}, f32[4,128,128]{2,1,0:T(8,128)S(1)}, f32[4,128,128]{2,1,0:T(8,128)S(1)}, f32[128,128]{1,0:T(8,128)S(1)}, /*index=5*/s32[]{:T(128)}) while((s32[]{:T(128)}, f32[4,128,128]{2,1,0:T(8,128)S(1)}, f32[4,128,128]{2,1,0:T(8,128)S(1)}, f32[4,128,128]{2,1,0:T(8,128)S(1)}, ...), condition=%wide.region_2.3_spmd, body=%wide.region_1.2_spmd.sunk | while | flops 35667968 | bytes 688205 | solution.py:105
  167.2 9.7 %fusion.107 = f32[128,1,128]{2,1,0:T(1,128)S(1)} fusion(f32[128,128,1]{1,2,0:T(1,128)S(1)} %bitcast.127, f32[128,128]{1,0:T(8,128)S(1)} %get-tuple-element.140, f32[128,128]{1,0:T(8,128)S(1)} %get-tuple-element.141, pred[128,128]{1,0:T(8,128)(4,1)S(1)} %iota_compare_fusion.10), kind=kOutput, calls=%fused_computation.1.clone.1 | convolution fusion | flops 35651584 | bytes 278528 | tf_op jit(solution)/shard_map/while/body/eval_jaxpr/ts,tsc,sc->tc/dot_general | solution.py:52
  177.0 9.7 %fusion.107 = f32[128,1,128]{2,1,0:T(1,128)S(1)} fusion(f32[128,128,1]{1,2,0:T(1,128)S(1)} %bitcast.127, f32[128,128]{1,0:T(8,128)S(1)} %get-tuple-element.140, f32[128,128]{1,0:T(8,128)S(1)} %get-tuple-element.141, pred[128,128]{1,0:T(8,128)(4,1)S(1)} %iota_compare_fusion.10), kind=kOutput, calls=%fused_computation.1.clone.1 | convolution fusion | flops 35651584 | bytes 278528 | tf_op jit(solution)/shard_map/while/body/eval_jaxpr/ts,tsc,sc->tc/dot_general | solution.py:52
  186.7 9.7 %fusion.107 = f32[128,1,128]{2,1,0:T(1,128)S(1)} fusion(f32[128,128,1]{1,2,0:T(1,128)S(1)} %bitcast.127, f32[128,128]{1,0:T(8,128)S(1)} %get-tuple-element.140, f32[128,128]{1,0:T(8,128)S(1)} %get-tuple-element.141, pred[128,128]{1,0:T(8,128)(4,1)S(1)} %iota_compare_fusion.10), kind=kOutput, calls=%fused_computation.1.clone.1 | convolution fusion | flops 35651584 | bytes 278528 | tf_op jit(solution)/shard_map/while/body/eval_jaxpr/ts,tsc,sc->tc/dot_general | solution.py:52
  196.5 9.7 %fusion.107 = f32[128,1,128]{2,1,0:T(1,128)S(1)} fusion(f32[128,128,1]{1,2,0:T(1,128)S(1)} %bitcast.127, f32[128,128]{1,0:T(8,128)S(1)} %get-tuple-element.140, f32[128,128]{1,0:T(8,128)S(1)} %get-tuple-element.141, pred[128,128]{1,0:T(8,128)(4,1)S(1)} %iota_compare_fusion.10), kind=kOutput, calls=%fused_computation.1.clone.1 | convolution fusion | flops 35651584 | bytes 278528 | tf_op jit(solution)/shard_map/while/body/eval_jaxpr/ts,tsc,sc->tc/dot_general | solution.py:52
  209.2 85.7 %while.21 = (s32[]{:T(128)}, f32[512,16]{0,1:T(8,128)S(1)}, f32[512]{0:T(512)S(1)}, f32[512,16]{0,1:T(8,128)S(1)}, s32[]{:T(128)}) while((s32[]{:T(128)}, f32[512,16]{0,1:T(8,128)S(1)}, f32[512]{0:T(512)S(1)}, f32[512,16]{0,1:T(8,128)S(1)}, s32[]{:T(128)}) %tuple.40), condition=%wide.region_4.5_spmd, body=%wide.region_3.4_spmd.sunk | while | flops 16386 | bytes 231525 | solution.py:118
  247.3 5.6 collective-permute-start
  254.1 5.6 collective-permute-start
  260.7 5.8 collective-permute-start
  267.5 5.8 collective-permute-start
  274.4 5.7 collective-permute-start
  281.0 5.8 collective-permute-start
  287.8 6.0 %collective-permute-start = (f32[512,16]{0,1:T(8,128)S(1)}, f32[512,16]{0,1:T(8,128)S(1)}, u32[]{:S(2)}, u32[]{:S(2)}) collective-permute-start(f32[512,16]{0,1:T(8,128)S(1)} %multiply_add_fusion.3), channel_id=1, source_target_pairs={{0,16},{16,32},{32,48},{48,64},{64,80},{80,96},{96,112},{112,128},... | collective-permute-start | bytes 98312 | tf_op jit(solution)/shard_map/while/body/eval_jaxpr/ppermute | solution.py:38
  300.1 83.1 %reduce-scatter.3.cloned.1.call-done = bf16[8,4096]{1,0:T(8,128)(2,1)} async-done(((bf16[128,4096]{1,0:T(8,128)(2,1)}), bf16[8,4096]{1,0:T(8,128)(2,1)}) %reduce-scatter.3.cloned.1.call-update) | async-done | bytes 65552 | tf_op jit(solution)/shard_map/reduce_scatter | solution.py:128
  384.6 19.1 %all_to_all.10 = bf16[16,2,4096]{2,1,0:T(2,128)(2,1)S(1)} all-to-all(bf16[16,2,4096]{2,1,0:T(2,128)(2,1)S(1)} %reshape.127), channel_id=1, replica_groups=mesh['ctx'=16,'exp'=16] {'exp'}, dimensions={0} | all-to-all | bytes 524288 | tf_op jit(solution)/shard_map/all_to_all | solution.py:162
  404.8 53.1 %all-gather.11.cloned.1.call-done = bf16[512,4096]{1,0:T(8,128)(2,1)} async-done(((bf16[32,4096]{1,0:T(8,128)(2,1)}), bf16[512,4096]{1,0:T(8,128)(2,1)}) %all-gather.11.cloned.1.call-update) | async-done | bytes 4194320 | tf_op jit(solution)/shard_map/all_gather | solution.py:167
  463.3 10.8 %convolution_convert_fusion = bf16[512,4096]{1,0:T(8,128)(2,1)} fusion(bf16[1,448,4096]{2,1,0:T(8,128)(2,1)} %param.32, bf16[512,4096]{1,0:T(8,128)(2,1)} %all-gather.11.cloned.1.call-done, bf16[1,448,4096]{2,1,0:T(8,128)(2,1)} %param.31, f32[512,448]{0,1:T(8,128)S(1)} %fusion.18), kind=kOutput, calls=%fused_computation.20 | convolution fusion | flops 3761569792 | bytes 16646144 | tf_op jit(solution)/shard_map/dot_general | solution.py:175
  474.1 80.9 %reduce-scatter.5.cloned.1.call-done = bf16[32,4096]{1,0:T(8,128)(2,1)} async-done(((bf16[512,4096]{1,0:T(8,128)(2,1)}), bf16[32,4096]{1,0:T(8,128)(2,1)}) %reduce-scatter.5.cloned.1.call-update) | async-done | bytes 262160 | tf_op jit(solution)/shard_map/reduce_scatter | solution.py:176
  556.9 9.4 %all-to-all-start.1 = ((bf16[16,2,4096]{2,1,0:T(2,128)(2,1)}), bf16[16,2,4096]{2,1,0:T(2,128)(2,1)S(1)}, u32[]{:S(2)}, u32[]{:S(2)}) async-start(bf16[16,2,4096]{2,1,0:T(2,128)(2,1)} %reshape.129), calls=%async_computation.3 | async-start | bytes 524288 | tf_op jit(solution)/shard_map/all_to_all | solution.py:179
  566.7 11.2 %all-to-all-done.1 = bf16[16,2,4096]{2,1,0:T(2,128)(2,1)S(1)} async-done(((bf16[16,2,4096]{2,1,0:T(2,128)(2,1)}), bf16[16,2,4096]{2,1,0:T(2,128)(2,1)S(1)}, u32[]{:S(2)}, u32[]{:S(2)}) %all-to-all-start.1) | async-done | bytes 262176 | tf_op jit(solution)/shard_map/all_to_all | solution.py:179
  (170 shorter events, 147.0 us)
Async XLA Ops:
  6.5 98.1 %all-gather.5.cloned.1.call-start = ((), (), s32[]{:S(2)}) async-start(), calls=%async_computation.4 | async-start | bytes 1114112 | tf_op jit(solution)/shard_map/all_gather | solution.py:72
  7.3 199.0 %all-gather.7.cloned.1.call-start = ((), (), s32[]{:S(2)}) async-start(), calls=%async_computation.5 | async-start | bytes 4456448 | tf_op jit(solution)/shard_map/all_gather | solution.py:80
  8.0 287.4 %all-gather.9.cloned.1.call-start = ((), (), s32[]{:S(2)}) async-start(), calls=%async_computation.6 | async-start | bytes 4456448 | tf_op jit(solution)/shard_map/all_gather | solution.py:127
  8.1 10.1 %collective-permute-start.1 = (bf16[256,512]{1,0:T(8,128)(2,1)}, bf16[256,512]{1,0:T(8,128)(2,1)S(1)}, u32[]{:S(2)}, u32[]{:S(2)}) collective-permute-start(bf16[256,512]{1,0:T(8,128)(2,1)} %param.20), channel_id=1, source_target_pairs={{0,16},{16,32},{32,48},{48,64},{64,80},{80,96},{96,112},{112,128},... | collective-permute-start | bytes 786440 | tf_op jit(solution)/shard_map/ppermute | solution.py:26
  18.2 8.5 %collective-permute-start.2 = (bf16[256,512]{1,0:T(8,128)(2,1)S(1)}, bf16[256,512]{1,0:T(8,128)(2,1)S(1)}, u32[]{:S(2)}, u32[]{:S(2)}) collective-permute-start(bf16[256,512]{1,0:T(8,128)(2,1)S(1)} %collective-permute-done.1), channel_id=1, source_target_pairs={{0,16},{16,32},{32,48},{48,64},{64,80},{80,96},{96,112},{112,128},... | collective-permute-start | bytes 786440 | tf_op jit(solution)/shard_map/ppermute | solution.py:26
  18.2 8.5 %collective-permute-start.9 = (bf16[256,512]{1,0:T(8,128)(2,1)}, bf16[256,512]{1,0:T(8,128)(2,1)S(1)}, u32[]{:S(2)}, u32[]{:S(2)}) collective-permute-start(bf16[256,512]{1,0:T(8,128)(2,1)} %param.20), channel_id=1, source_target_pairs={{16,0},{32,16},{48,32},{64,48},{80,64},{96,80},{112,96},{128,112},... | collective-permute-start | bytes 786440 | tf_op jit(solution)/shard_map/ppermute | solution.py:28
  26.7 8.5 %collective-permute-start.3 = (bf16[256,512]{1,0:T(8,128)(2,1)S(1)}, bf16[256,512]{1,0:T(8,128)(2,1)S(1)}, u32[]{:S(2)}, u32[]{:S(2)}) collective-permute-start(bf16[256,512]{1,0:T(8,128)(2,1)S(1)} %collective-permute-done.2), channel_id=1, source_target_pairs={{0,16},{16,32},{32,48},{48,64},{64,80},{80,96},{96,112},{112,128},... | collective-permute-start | bytes 786440 | tf_op jit(solution)/shard_map/ppermute | solution.py:26
  26.7 8.5 %collective-permute-start.10 = (bf16[256,512]{1,0:T(8,128)(2,1)S(1)}, bf16[256,512]{1,0:T(8,128)(2,1)S(1)}, u32[]{:S(2)}, u32[]{:S(2)}) collective-permute-start(bf16[256,512]{1,0:T(8,128)(2,1)S(1)} %collective-permute-done.9), channel_id=1, source_target_pairs={{16,0},{32,16},{48,32},{64,48},{80,64},{96,80},{112,96},{128,112},... | collective-permute-start | bytes 786440 | tf_op jit(solution)/shard_map/ppermute | solution.py:28
  35.3 8.5 %collective-permute-start.4 = (bf16[256,512]{1,0:T(8,128)(2,1)S(1)}, bf16[256,512]{1,0:T(8,128)(2,1)S(1)}, u32[]{:S(2)}, u32[]{:S(2)}) collective-permute-start(bf16[256,512]{1,0:T(8,128)(2,1)S(1)} %collective-permute-done.3), channel_id=1, source_target_pairs={{0,16},{16,32},{32,48},{48,64},{64,80},{80,96},{96,112},{112,128},... | collective-permute-start | bytes 786440 | tf_op jit(solution)/shard_map/ppermute | solution.py:26
  35.3 8.5 %collective-permute-start.11 = (bf16[256,512]{1,0:T(8,128)(2,1)S(1)}, bf16[256,512]{1,0:T(8,128)(2,1)S(1)}, u32[]{:S(2)}, u32[]{:S(2)}) collective-permute-start(bf16[256,512]{1,0:T(8,128)(2,1)S(1)} %collective-permute-done.10), channel_id=1, source_target_pairs={{16,0},{32,16},{48,32},{64,48},{80,64},{96,80},{112,96},{128,112},... | collective-permute-start | bytes 786440 | tf_op jit(solution)/shard_map/ppermute | solution.py:28
  43.8 8.8 %collective-permute-start.5 = (bf16[256,512]{1,0:T(8,128)(2,1)S(1)}, bf16[256,512]{1,0:T(8,128)(2,1)S(1)}, u32[]{:S(2)}, u32[]{:S(2)}) collective-permute-start(bf16[256,512]{1,0:T(8,128)(2,1)S(1)} %collective-permute-done.4), channel_id=1, source_target_pairs={{0,16},{16,32},{32,48},{48,64},{64,80},{80,96},{96,112},{112,128},... | collective-permute-start | bytes 786440 | tf_op jit(solution)/shard_map/ppermute | solution.py:26
  43.8 8.8 %collective-permute-start.12 = (bf16[256,512]{1,0:T(8,128)(2,1)S(1)}, bf16[256,512]{1,0:T(8,128)(2,1)S(1)}, u32[]{:S(2)}, u32[]{:S(2)}) collective-permute-start(bf16[256,512]{1,0:T(8,128)(2,1)S(1)} %collective-permute-done.11), channel_id=1, source_target_pairs={{16,0},{32,16},{48,32},{64,48},{80,64},{96,80},{112,96},{128,112},... | collective-permute-start | bytes 786440 | tf_op jit(solution)/shard_map/ppermute | solution.py:28
  52.6 9.8 %collective-permute-start.6 = (bf16[256,512]{1,0:T(8,128)(2,1)S(1)}, bf16[256,512]{1,0:T(8,128)(2,1)S(1)}, u32[]{:S(2)}, u32[]{:S(2)}) collective-permute-start(bf16[256,512]{1,0:T(8,128)(2,1)S(1)} %collective-permute-done.5), channel_id=1, source_target_pairs={{0,16},{16,32},{32,48},{48,64},{64,80},{80,96},{96,112},{112,128},... | collective-permute-start | bytes 786440 | tf_op jit(solution)/shard_map/ppermute | solution.py:26
  52.6 330.5 %reduce-scatter.3.cloned.1.call-start = ((), (), s32[]{:S(2)}) async-start(), calls=%async_computation.7 | async-start | bytes 1114112 | tf_op jit(solution)/shard_map/reduce_scatter | solution.py:128
  52.7 10.1 %collective-permute-start.13 = (bf16[256,512]{1,0:T(8,128)(2,1)S(1)}, bf16[256,512]{1,0:T(8,128)(2,1)S(1)}, u32[]{:S(2)}, u32[]{:S(2)}) collective-permute-start(bf16[256,512]{1,0:T(8,128)(2,1)S(1)} %collective-permute-done.12), channel_id=1, source_target_pairs={{16,0},{32,16},{48,32},{64,48},{80,64},{96,80},{112,96},{128,112},... | collective-permute-start | bytes 786440 | tf_op jit(solution)/shard_map/ppermute | solution.py:28
  62.4 13.8 %collective-permute-start.7 = (bf16[256,512]{1,0:T(8,128)(2,1)S(1)}, bf16[256,512]{1,0:T(8,128)(2,1)S(1)}, u32[]{:S(2)}, u32[]{:S(2)}) collective-permute-start(bf16[256,512]{1,0:T(8,128)(2,1)S(1)} %collective-permute-done.6), channel_id=1, source_target_pairs={{0,16},{16,32},{32,48},{48,64},{64,80},{80,96},{96,112},{112,128},... | collective-permute-start | bytes 786440 | tf_op jit(solution)/shard_map/ppermute | solution.py:26
  62.8 14.3 %collective-permute-start.14 = (bf16[256,512]{1,0:T(8,128)(2,1)S(1)}, bf16[256,512]{1,0:T(8,128)(2,1)S(1)}, u32[]{:S(2)}, u32[]{:S(2)}) collective-permute-start(bf16[256,512]{1,0:T(8,128)(2,1)S(1)} %collective-permute-done.13), channel_id=1, source_target_pairs={{16,0},{32,16},{48,32},{64,48},{80,64},{96,80},{112,96},{128,112},... | collective-permute-start | bytes 786440 | tf_op jit(solution)/shard_map/ppermute | solution.py:28
  76.2 11.8 %collective-permute-start.8 = (bf16[256,512]{1,0:T(8,128)(2,1)S(1)}, bf16[256,512]{1,0:T(8,128)(2,1)S(1)}, u32[]{:S(2)}, u32[]{:S(2)}) collective-permute-start(bf16[256,512]{1,0:T(8,128)(2,1)S(1)} %collective-permute-done.7), channel_id=1, source_target_pairs={{0,16},{16,32},{32,48},{48,64},{64,80},{80,96},{96,112},{112,128},... | collective-permute-start | bytes 786440 | tf_op jit(solution)/shard_map/ppermute | solution.py:26
  77.1 21.8 %collective-permute-start.15 = (bf16[256,512]{1,0:T(8,128)(2,1)S(1)}, bf16[256,512]{1,0:T(8,128)(2,1)S(1)}, u32[]{:S(2)}, u32[]{:S(2)}) collective-permute-start(bf16[256,512]{1,0:T(8,128)(2,1)S(1)} %collective-permute-done.14), channel_id=1, source_target_pairs={{16,0},{32,16},{48,32},{64,48},{80,64},{96,80},{112,96},{128,112},... | collective-permute-start | bytes 786440 | tf_op jit(solution)/shard_map/ppermute | solution.py:28
  267.5 6.9 %collective-permute-start = (f32[512,16]{0,1:T(8,128)S(1)}, f32[512,16]{0,1:T(8,128)S(1)}, u32[]{:S(2)}, u32[]{:S(2)}) collective-permute-start(f32[512,16]{0,1:T(8,128)S(1)} %multiply_add_fusion.3), channel_id=1, source_target_pairs={{0,16},{16,32},{32,48},{48,64},{64,80},{80,96},{96,112},{112,128},... | collective-permute-start | bytes 98312 | tf_op jit(solution)/shard_map/while/body/eval_jaxpr/ppermute | solution.py:38
  287.8 7.1 %collective-permute-start = (f32[512,16]{0,1:T(8,128)S(1)}, f32[512,16]{0,1:T(8,128)S(1)}, u32[]{:S(2)}, u32[]{:S(2)}) collective-permute-start(f32[512,16]{0,1:T(8,128)S(1)} %multiply_add_fusion.3), channel_id=1, source_target_pairs={{0,16},{16,32},{32,48},{48,64},{64,80},{80,96},{96,112},{112,128},... | collective-permute-start | bytes 98312 | tf_op jit(solution)/shard_map/while/body/eval_jaxpr/ppermute | solution.py:38
  299.3 158.6 %all-gather.11.cloned.1.call-start = ((), (), s32[]{:S(2)}) async-start(), calls=%async_computation.8 | async-start | bytes 4456448 | tf_op jit(solution)/shard_map/all_gather | solution.py:167
  404.5 150.5 %reduce-scatter.5.cloned.1.call-start = ((), (), s32[]{:S(2)}) async-start(), calls=%async_computation.9 | async-start | bytes 4456448 | tf_op jit(solution)/shard_map/reduce_scatter | solution.py:176
  556.9 21.1 %all-to-all-start.1 = ((bf16[16,2,4096]{2,1,0:T(2,128)(2,1)}), bf16[16,2,4096]{2,1,0:T(2,128)(2,1)S(1)}, u32[]{:S(2)}, u32[]{:S(2)}) async-start(bf16[16,2,4096]{2,1,0:T(2,128)(2,1)} %reshape.129), calls=%async_computation.3 | async-start | bytes 524288 | tf_op jit(solution)/shard_map/all_to_all | solution.py:179
  (23 other events, 541.7 us)
Sparse Core Ops, SparseCore 0:
  9.1 41.7 all-gather.4
  53.3 61.6 all-gather.6
  117.4 62.0 all-gather.8
  299.5 83.5 reduce-scatter.2
  404.7 53.1 all-gather.10
  474.3 80.7 reduce-scatter.4
